TPU v7x, 256 devices: a whole 4x4x8 slice. The times are simulated.
256 devices in a mesh: cfg: 2 (over x_hi), seq: 64 (over x_lo, z, y), clip: 2 (over core).
Axes of the slice: x: 4 (x_hi: 2, x_lo: 2; x = x_hi * 2 + x_lo), y: 4, z: 8, core: 2. Of those that a mesh axis runs over, the one named last changes fastest.
Arguments:
- clean: bfloat16 [128, 256, 1152], P(('clip', 'seq')), parts along dimension 0, may hold values from -6 to 6
- noise: bfloat16 [128, 256, 1152], P(('clip', 'seq')), parts along dimension 0, may hold values from -6 to 6
- timestep: float32 [2], P('clip'), parts along dimension 0, may hold values from 0.1 to 0.9
- guidance: float32 [2], P('clip'), parts along dimension 0, may hold values from 2 to 6
- condition_vector: bfloat16 [2304], P('clip'), parts along dimension 0, may hold values from -6 to 6
- empty_prompt_vector: bfloat16 [1152], replicated, may hold values from -6 to 6
- timestep_direction: bfloat16 [1152], replicated, may hold values from -6 to 6
- spatial_query_key_value: bfloat16 [3, 1152, 1152], P(None, None, ('cfg', 'seq')), may hold values from -1 to 1
- spatial_output_weight: bfloat16 [1152, 1152], P(('cfg', 'seq')), may hold values from -0.1875 to 0.1875
- temporal_query_key_value: bfloat16 [3, 1152, 1152], P(None, None, ('cfg', 'seq')), may hold values from -1 to 1
- temporal_output_weight: bfloat16 [1152, 1152], P(('cfg', 'seq')), may hold values from -0.1875 to 0.1875
- adapter_down_maps: bfloat16 [2, 1152, 64], replicated, may hold values from -0.1875 to 0.1875
- adapter_up_maps: bfloat16 [2, 64, 1152], replicated, may hold values from -0.75 to 0.75
Outputs:
- student_out: bfloat16 [128, 256, 1152], P(('clip', 'seq'), 'cfg'), parts along dimension 0
- student_tangent: bfloat16 [128, 256, 1152], P(('clip', 'seq'), 'cfg'), parts along dimension 0
There are 2 independent parts, one for each index of `clip`. A program takes and returns all parts, laid end to end along the dimension named above; an argument that names none is the same for every part. Nothing has to cross between parts.
All inputs are finite; a program needn't handle non-finite values.
Results may differ from a plain program's by a relative error of at most 0.028.
Values may be sent and summed in bfloat16 or wider, within the bound.
A program may use at most 128 MiB of HBM per device.

v0:
```python
import jax
import jax.numpy as jnp
from jax import lax
from jax.sharding import PartitionSpec as P

HEAD_DIM = 72
epsilon = 1e-06


def partner(value, axis, bit):
    mask = 2**bit
    pairs = [(source, source ^ mask) for source in range(lax.axis_size(axis))]
    return lax.ppermute(value, axis, pairs)


def rms_scale(features):
    return features * lax.rsqrt(jnp.mean(features * features, axis=-1, keepdims=True) + epsilon)


def project(rows_in, matrix):
    return jnp.einsum("...d,dk->...k", rows_in, matrix, preferred_element_type=jnp.float32)


def space_attend(queries, key_rows, value_rows):
    head_count = queries.shape[-1] // HEAD_DIM
    split_dims = queries.shape[:-1] + (head_count, HEAD_DIM)
    scores = jnp.einsum(
        "...qhd,...khd->...hqk",
        queries.reshape(split_dims),
        key_rows.reshape(split_dims),
        preferred_element_type=jnp.float32,
    ) * HEAD_DIM ** (-0.5)
    scores = scores - jnp.max(scores, axis=-1, keepdims=True)
    exponent = jnp.exp(scores)
    soft_weights = (exponent / jnp.sum(exponent, axis=-1, keepdims=True)).astype(jnp.bfloat16)
    result = jnp.einsum(
        "...hqk,...khd->...qhd",
        soft_weights,
        value_rows.reshape(split_dims),
        preferred_element_type=jnp.float32,
    )
    return result.astype(jnp.bfloat16).reshape(queries.shape)


def time_attend(queries, key_rows, value_rows):
    head_count = queries.shape[-1] // HEAD_DIM
    split_dims = queries.shape[:-1] + (head_count, HEAD_DIM)
    scores = jnp.einsum(
        "...fxhd,...gxhd->...xhfg",
        queries.reshape(split_dims),
        key_rows.reshape(split_dims),
        preferred_element_type=jnp.float32,
    ) * HEAD_DIM ** (-0.5)
    scores = scores - jnp.max(scores, axis=-1, keepdims=True)
    exponent = jnp.exp(scores)
    soft_weights = (exponent / jnp.sum(exponent, axis=-1, keepdims=True)).astype(jnp.bfloat16)
    result = jnp.einsum(
        "...xhfg,...gxhd->...fxhd",
        soft_weights,
        value_rows.reshape(split_dims),
        preferred_element_type=jnp.float32,
    )
    return result.astype(jnp.bfloat16).reshape(queries.shape)


def time_core(embedding_rows, query_weight, key_weight, value_weight, out_weight):
    normed = rms_scale(embedding_rows).astype(jnp.bfloat16)
    queries = project(normed, query_weight).astype(jnp.bfloat16)
    key_rows = project(normed, key_weight).astype(jnp.bfloat16)
    value_rows = project(normed, value_weight).astype(jnp.bfloat16)
    return project(time_attend(queries, key_rows, value_rows), out_weight)


def student_network(
    embedding_rows,
    query_weight,
    key_weight,
    value_weight,
    out_weight,
    down_query,
    query_up_map,
    down_value,
    value_up_map,
):
    normed = rms_scale(embedding_rows).astype(jnp.bfloat16)
    low_query = project(normed, down_query).astype(jnp.bfloat16)
    low_value = project(normed, down_value).astype(jnp.bfloat16)
    queries = (project(normed, query_weight) + project(low_query, query_up_map)).astype(
        jnp.bfloat16
    )
    key_rows = project(normed, key_weight).astype(jnp.bfloat16)
    value_rows = (project(normed, value_weight) + project(low_value, value_up_map)).astype(
        jnp.bfloat16
    )
    return project(time_attend(queries, key_rows, value_rows), out_weight)


def on_device(
    clean,
    noise,
    timestep,
    guidance,
    condition_vector,
    empty_prompt_vector,
    timestep_direction,
    spatial_query_key_value,
    spatial_output_weight,
    temporal_query_key_value,
    temporal_output_weight,
    adapter_down_maps,
    adapter_up_maps,
):
    moment = timestep[0]
    strength = guidance[0]
    pair_side = lax.axis_index("cfg")
    noisy_rows = (
        (1.0 - moment) * clean.astype(jnp.float32) + moment * noise.astype(jnp.float32)
    ).astype(jnp.bfloat16)
    shifted = noisy_rows.astype(jnp.float32) + moment * timestep_direction.astype(jnp.float32)
    embeds = jnp.where(pair_side == 0, condition_vector, empty_prompt_vector)[None]
    branch_count = embeds.shape[0]
    entries = shifted[None] + embeds.astype(jnp.float32)[:, None, None, :]
    normed = rms_scale(entries).astype(jnp.bfloat16)
    triple = jnp.einsum(
        "bfpd,jdk->jbfpk",
        normed,
        lax.all_gather(spatial_query_key_value, ("cfg", "seq"), axis=2, tiled=True),
        preferred_element_type=jnp.float32,
    ).astype(jnp.bfloat16)
    attended = space_attend(triple[0], triple[1], triple[2])
    partial_value = jnp.einsum(
        "bfpk,kd->bfpd",
        attended,
        lax.all_gather(spatial_output_weight, ("cfg", "seq"), axis=0, tiled=True),
        preferred_element_type=jnp.float32,
    )
    layer_one = (entries + partial_value).astype(jnp.bfloat16)
    frame_count = layer_one.shape[1]
    position_count = layer_one.shape[2]
    width = layer_one.shape[3]
    stacked = jnp.concatenate([layer_one, noisy_rows[None]], axis=0).reshape(
        branch_count + 1, frame_count, 2, position_count // 2, width
    )
    regrouped = lax.all_to_all(stacked, "seq", split_axis=3, concat_axis=1, tiled=True)
    frames = regrouped.shape[1]
    local_rows = regrouped.shape[3]
    teacher_in = regrouped[:branch_count].reshape(branch_count, frames, 2 * local_rows, width)
    noisy_local = regrouped[branch_count]
    time_qkv, time_out = (
        lax.all_gather(temporal_query_key_value, ("cfg", "seq"), axis=2, tiled=True),
        lax.all_gather(temporal_output_weight, ("cfg", "seq"), axis=0, tiled=True),
    )
    teacher_part = time_core(
        teacher_in.astype(jnp.float32), time_qkv[0], time_qkv[1], time_qkv[2], time_out
    )
    velocity = (
        (teacher_in.astype(jnp.float32) + teacher_part)
        .astype(jnp.bfloat16)
        .reshape(branch_count, frames, 2, local_rows, width)
    )
    own_velocity = velocity[0]
    own_half = lax.dynamic_index_in_dim(own_velocity, pair_side, 1, keepdims=False)
    outgoing = lax.dynamic_index_in_dim(own_velocity, 1 - pair_side, 1, keepdims=False)
    other_half = partner(outgoing, "cfg", 0)
    is_first = pair_side == 0
    cond_velocity = jnp.where(is_first, own_half, other_half)
    uncond_velocity = jnp.where(is_first, other_half, own_half)
    student_noisy = lax.dynamic_index_in_dim(noisy_local, pair_side, 1, keepdims=False)
    query_up_map = adapter_up_maps[0]
    value_up_map = adapter_up_maps[1]
    uncond_float = uncond_velocity.astype(jnp.float32)
    guided = (uncond_float + strength * (cond_velocity.astype(jnp.float32) - uncond_float)).astype(
        jnp.bfloat16
    )
    student_in = (
        student_noisy.astype(jnp.float32)
        + moment * timestep_direction.astype(jnp.float32)
        + condition_vector.astype(jnp.float32)
    )

    def student_map(embedding_rows):
        return student_network(
            embedding_rows,
            time_qkv[0],
            time_qkv[1],
            time_qkv[2],
            time_out,
            adapter_down_maps[0],
            query_up_map,
            adapter_down_maps[1],
            value_up_map,
        )

    partial_value, tangent_part = jax.jvp(student_map, (student_in,), (guided.astype(jnp.float32),))
    primal = (student_in + partial_value).astype(jnp.bfloat16)
    tangent = (guided.astype(jnp.float32) + tangent_part).astype(jnp.bfloat16)
    returned = lax.all_to_all(
        jnp.stack([primal, tangent]), "seq", split_axis=1, concat_axis=2, tiled=True
    )
    return (returned[0], returned[1])


def solution(mesh):
    return jax.shard_map(
        on_device,
        mesh=mesh,
        in_specs=(
            P(("clip", "seq"), None, None),
            P(("clip", "seq"), None, None),
            P("clip"),
            P("clip"),
            P("clip"),
            P(),
            P(),
            P(None, None, ("cfg", "seq")),
            P(("cfg", "seq"), None),
            P(None, None, ("cfg", "seq")),
            P(("cfg", "seq"), None),
            P(),
            P(),
        ),
        out_specs=(P(("clip", "seq"), "cfg", None), P(("clip", "seq"), "cfg", None)),
        check_vma=False,
    )
```

profile of v0, /device:TPU:32, one launch (start us, length us, event | category | flops | bytes accessed | tf_op | source)
XLA Modules:
  0.0 703.8 jit_solution(14930948228672094972)
XLA Ops:
  15.2 115.8 %all-gather.11.cloned.1.call-done = bf16[128,9,1152]{2,1,0:T(8,128)(2,1)} async-done(((bf16[1,9,1152]{2,1,0:T(8,128)(2,1)}), bf16[128,9,1152]{2,1,0:T(8,128)(2,1)}) %all-gather.11.cloned.1.call-update) | async-done | bytes 2654224 | tf_op jit(solution)/shard_map/all_gather | solution.py:134
  131.0 4.3 reshape.305
  135.3 113.3 %all-gather.13.cloned.1.call-done = bf16[128,9,1152]{2,1,0:T(8,128)(2,1)} async-done(((bf16[1,9,1152]{2,1,0:T(8,128)(2,1)}), bf16[128,9,1152]{2,1,0:T(8,128)(2,1)}) %all-gather.13.cloned.1.call-update) | async-done | bytes 2654224 | tf_op jit(solution)/shard_map/all_gather | solution.py:151
  248.6 5.7 reshape.316
  254.4 124.3 %all-gather.7.cloned.1.call-done = bf16[3,1152,1152]{1,0,2:T(4,128)(2,1)} async-done(((bf16[3,1152,9]{1,0,2:T(4,128)(2,1)}), bf16[3,1152,1152]{1,0,2:T(4,128)(2,1)}) %all-gather.7.cloned.1.call-update) | async-done | bytes 7962640 | tf_op jit(solution)/shard_map/all_gather | solution.py:127
  378.7 6.6 fusion.10
  391.9 4.9 fusion.164
  396.8 2.8 fusion.61
  401.3 2.6 pad_maximum_fusion
  403.9 8.9 %all-to-all-start = ((bf16[2,1,2,128,1152]{4,2,0,1,3:T(2,128)(2,1)}), bf16[2,1,2,128,1152]{4,2,0,1,3:T(2,128)(2,1)}, u32[]{:S(2)}, u32[]{:S(2)}) async-start(bf16[2,1,2,128,1152]{4,2,0,1,3:T(2,128)(2,1)} %pad_maximum_fusion), calls=%async_computation | async-start | bytes 2359296 | tf_op jit(solution)/shard_map/all_to_all | solution.py:144
  412.7 98.1 %all-gather.9.cloned.1.call-done = bf16[3,1152,1152]{1,0,2:T(4,128)(2,1)} async-done(((bf16[3,1152,9]{1,0,2:T(4,128)(2,1)}), bf16[3,1152,1152]{1,0,2:T(4,128)(2,1)}) %all-gather.9.cloned.1.call-update) | async-done | bytes 7962640 | tf_op jit(solution)/shard_map/all_gather | solution.py:150
  510.9 24.1 %fusion.161 = (bf16[1,1152,1152]{1,0,2:T(2,128)(2,1)}, bf16[1,1152,1152]{1,0,2:T(2,128)(2,1)}, bf16[1,1152,1152]{1,0,2:T(2,128)(2,1)}) fusion(bf16[3,1152,1152]{1,0,2:T(4,128)(2,1)} %all-gather.9.cloned.1.call-done), kind=kLoop, calls=%fused_computation.171 | loop fusion | bytes 15925248 | tf_op jit(solution)/shard_map/jvp()/slice | solution.py:184
  535.0 10.9 %copy.107 = bf16[1,1152,1152]{2,1,0:T(8,128)(2,1)S(1)} copy(bf16[1,1152,1152]{1,0,2:T(2,128)(2,1)} %get-tuple-element.11) | data formatting | bytes 5308416
  545.8 12.2 %copy.108 = bf16[1,1152,1152]{2,1,0:T(8,128)(2,1)} copy(bf16[1,1152,1152]{1,0,2:T(2,128)(2,1)} %get-tuple-element.13) | data formatting | bytes 5308416
  558.1 12.2 %copy.106 = bf16[1,1152,1152]{2,1,0:T(8,128)(2,1)} copy(bf16[1,1152,1152]{1,0,2:T(2,128)(2,1)} %get-tuple-element.12) | data formatting | bytes 5308416
  574.8 2.8 reshape.295
  577.6 2.9 fusion.37
  580.5 2.8 reshape.296
  583.3 3.6 fusion.66
  586.9 2.6 fusion.165
  589.5 2.5 slice_convert_fusion
  592.1 2.9 fusion.31
  595.0 3.7 reshape.294
  598.7 3.9 fusion.59
  602.6 2.9 copy.88
  605.5 2.9 reshape.297
  608.4 3.2 fusion.41
  613.2 3.1 collective-permute-start
  616.9 5.5 collective-permute-done
  623.8 3.4 fusion.29
  655.0 2.3 fusion.55
  667.6 27.1 %all_to_all.24 = bf16[2,64,2,1152]{3,2,0,1:T(2,128)(2,1)S(1)} all-to-all(bf16[2,64,2,1152]{3,2,0,1:T(2,128)(2,1)S(1)} %copy.98), channel_id=1, replica_groups=mesh['cfg'=2,'seq'=64,'clip'=2] {'seq'}, dimensions={1} | all-to-all | bytes 1179648 | tf_op jit(solution)/shard_map/all_to_all | solution.py:197
  (135 shorter events, 62.8 us)
Async XLA Ops:
  7.2 123.8 %all-gather.11.cloned.1.call-start = ((), (), s32[]{:S(2)}) async-start(), calls=%async_computation.4 | async-start | bytes 4755456 | tf_op jit(solution)/shard_map/all_gather | solution.py:134
  7.9 240.7 %all-gather.13.cloned.1.call-start = ((), (), s32[]{:S(2)}) async-start(), calls=%async_computation.5 | async-start | bytes 4755456 | tf_op jit(solution)/shard_map/all_gather | solution.py:151
  8.6 370.0 %all-gather.7.cloned.1.call-start = ((), (), s32[]{:S(2)}) async-start(), calls=%async_computation.2 | async-start | bytes 10699776 | tf_op jit(solution)/shard_map/all_gather | solution.py:127
  9.4 501.5 %all-gather.9.cloned.1.call-start = ((), (), s32[]{:S(2)}) async-start(), calls=%async_computation.3 | async-start | bytes 10699776 | tf_op jit(solution)/shard_map/all_gather | solution.py:150
  13.8 364.9 %copy-start.15 = (bf16[1,256,1152]{2,1,0:T(8,128)(2,1)}, bf16[1,256,1152]{2,1,0:T(8,128)(2,1)S(1)}, u32[]{:S(2)}) copy-start(bf16[1,256,1152]{2,1,0:T(8,128)(2,1)S(1)} %get-tuple-element.10) | copy-start | bytes 1769476
  391.9 4.9 copy-start.22
  396.8 2.8 copy-start.16
  399.6 1.7 copy-start.14
  403.9 166.4 %all-to-all-start = ((bf16[2,1,2,128,1152]{4,2,0,1,3:T(2,128)(2,1)}), bf16[2,1,2,128,1152]{4,2,0,1,3:T(2,128)(2,1)}, u32[]{:S(2)}, u32[]{:S(2)}) async-start(bf16[2,1,2,128,1152]{4,2,0,1,3:T(2,128)(2,1)} %pad_maximum_fusion), calls=%async_computation | async-start | bytes 2359296 | tf_op jit(solution)/shard_map/all_to_all | solution.py:144
  589.5 2.6 copy-start
  613.2 9.2 %collective-permute-start = (bf16[64,2,1152]{2,0,1:T(8,128)(2,1)}, bf16[64,2,1152]{2,0,1:T(8,128)(2,1)S(1)}, u32[]{:S(2)}, u32[]{:S(2)}) collective-permute-start(bf16[64,2,1152]{2,0,1:T(8,128)(2,1)} %dynamic-slice_bitcast_fusion), channel_id=1, source_target_pairs={{0,128},{128,0},{1,129},{129,1},{2,130},{130,2},{3,131},{131,3},{4... | collective-permute-start | bytes 884744 | tf_op jit(solution)/shard_map/ppermute | solution.py:13
  623.8 3.4 copy-start.9
  623.8 7.6 %copy-start.27 = (f32[64,2]{0,1:T(2,128)}, f32[64,2]{0,1:T(2,128)S(1)}, u32[]{:S(2)}) copy-start(f32[64,2]{0,1:T(2,128)S(1)} %get-tuple-element.23) | copy-start | bytes 1540
  623.8 3.6 copy-start.2
  631.4 2.0 copy-start.1
  634.8 4.3 copy-start.13
  637.2 7.1 %copy-start.11 = (f32[64,2,1152]{2,0,1:T(8,128)S(1)}, f32[64,2,1152]{2,0,1:T(8,128)}, u32[]{:S(2)}) copy-start(f32[64,2,1152]{2,0,1:T(8,128)} %fusion.23) | copy-start | bytes 1769476
  648.5 2.6 copy-start.7
  648.6 2.6 copy-start.25
  649.0 2.1 copy-start.23
  649.4 2.1 copy-start.29
  651.1 3.9 copy-start.3
  657.2 3.7 copy-start.26
  657.2 3.7 copy-start.32
  661.0 2.0 copy-start.33
  661.0 2.0 copy-start.6
  661.0 2.0 copy-start.8
  661.0 2.1 copy-start.24
  661.0 2.1 copy-start.30
  661.0 2.1 copy-start.34
  663.1 2.2 copy-start.10
  665.3 1.6 copy-start.19
  (9 other events, 11.0 us)
Sparse Core Ops, SparseCore 0:
  11.7 119.2 all-gather.10
  134.7 113.9 all-gather.12
  252.2 126.4 all-gather.6
  382.1 128.6 all-gather.8
where the time goes:
time: 714 us; the launch traced here: 704 us
  waiting for transfers between devices  460 us (64%)
  local copies, waits for them, and re-layouts  116 us (16%)
  matrix products  60.1 us (8%)
  blocking collectives  27.1 us (4%)
  between operations  16 us (2%)
  other arithmetic  12.3 us (2%)
  starting transfers between devices  12.1 us (2%)
    all_gather x1, waiting for transfers between devices, on_device(): lax.all_gather(spatial_query_key_value, ('cfg', 'seq'), axis=2, tiled=True)  124 us
    all_gather x1, waiting for transfers between devices, on_device(): lax.all_gather(spatial_output_weight, ('cfg', 'seq'), axis=0, tiled=True)  116 us
    all_gather x1, waiting for transfers between devices, on_device(): lax.all_gather(temporal_output_weight, ('cfg', 'seq'), axis=0, tiled=True)  113 us
    all_gather x1, waiting for transfers between devices, on_device(): lax.all_gather(temporal_query_key_value, ('cfg', 'seq'), axis=2, tiled=True)  98.1 us
    unnamed x75, local copies, waits for them, and re-layouts  48.6 us
    dot_general x16, matrix products, project(): jnp.einsum('...d,dk->...k', rows_in, matrix, preferred_element_type=jnp.f...  29.4 us
    all_to_all x1, blocking collectives, on_device(): lax.all_to_all(jnp.stack([primal, tangent]), 'seq', split_axis=1, concat_...  27.1 us
    slice x1, local copies, waits for them, and re-layouts, student_map(): time_qkv[0]  24.1 us
  transfers between devices with their start and end apart: 6, of which 5 were waited for; matrix products, arithmetic and copies ran while one was open for 14% of the time, Pallas kernels for 0%

commit v1 on v0

--- a/solution.py
+++ b/solution.py
@@ -124,7 +124,15 @@
     triple = jnp.einsum(
         "bfpd,jdk->jbfpk",
         normed,
-        lax.all_gather(spatial_query_key_value, ("cfg", "seq"), axis=2, tiled=True),
+        jnp.concatenate(
+            lax.all_to_all(
+                jnp.stack([spatial_query_key_value] * lax.axis_size(("cfg", "seq"))),
+                ("cfg", "seq"),
+                0,
+                0,
+            ),
+            axis=2,
+        ),
         preferred_element_type=jnp.float32,
     ).astype(jnp.bfloat16)
     attended = space_attend(triple[0], triple[1], triple[2])

time: 714 us -> 658 us (0.922)
  waiting for transfers between devices: 460 us -> 391 us
  starting transfers between devices: 12.1 us -> 28.1 us
    all_gather x1 -> x0, waiting for transfers between devices: 124 us -> none  [on_device(): lax.all_gather(spatial_query_key_value, ('cfg', 'seq'), axis=2, tiled=True)]
    all_gather x1, waiting for transfers between devices: 116 us -> 158 us  [on_device(): lax.all_gather(spatial_output_weight, ('cfg', 'seq'), axis=0, tiled=True)]
    all_gather x1, waiting for transfers between devices: 113 us -> 133 us  [on_device(): lax.all_gather(temporal_output_weight, ('cfg', 'seq'), axis=0, tiled=True)]
    all_to_all x0 -> x1, starting transfers between devices: none -> 15.5 us  [on_device(): lax.all_to_all(jnp.stack([spatial_query_key_value] * lax.axis_size(('cfg'...]
    another operation x4 -> x5, local copies, waits for them, and re-layouts: 12.3 us -> 17.6 us
    unnamed x75 -> x85, local copies, waits for them, and re-layouts: 48.6 us -> 48.6 us
  transfers between devices with their start and end apart: 6 -> 6, of which waited for: 5 -> 4; matrix products, arithmetic and copies ran while one was open for 14% -> 16% of each run, Pallas kernels for 0% -> 0%
where the time goes in v1:
time: 658 us; the launch traced here: 654 us
  waiting for transfers between devices  391 us (59%)
  local copies, waits for them, and re-layouts  122 us (19%)
  matrix products  60 us (9%)
  starting transfers between devices  28.1 us (4%)
  blocking collectives  27.2 us (4%)
  between operations  15.9 us (2%)
  other arithmetic  9.71 us (1%)
    all_gather x1, waiting for transfers between devices, on_device(): lax.all_gather(spatial_output_weight, ('cfg', 'seq'), axis=0, tiled=True)  158 us
    all_gather x1, waiting for transfers between devices, on_device(): lax.all_gather(temporal_output_weight, ('cfg', 'seq'), axis=0, tiled=True)  133 us
    all_gather x1, waiting for transfers between devices, on_device(): lax.all_gather(temporal_query_key_value, ('cfg', 'seq'), axis=2, tiled=True)  92.9 us
    unnamed x85, local copies, waits for them, and re-layouts  48.6 us
    dot_general x16, matrix products, project(): jnp.einsum('...d,dk->...k', rows_in, matrix, preferred_element_type=jnp.f...  29.4 us
    all_to_all x1, blocking collectives, on_device(): lax.all_to_all(jnp.stack([primal, tangent]), 'seq', split_axis=1, concat_...  27.2 us
    slice x1, local copies, waits for them, and re-layouts, student_map(): time_qkv[0]  24 us
    all_to_all x1, starting transfers between devices, on_device(): lax.all_to_all(jnp.stack([spatial_query_key_value] * lax.axis_size(('cfg'...  15.5 us
  transfers between devices with their start and end apart: 6, of which 4 were waited for; matrix products, arithmetic and copies ran while one was open for 16% of the time, Pallas kernels for 0%

profile of v1, /device:TPU:32, one launch (start us, length us, event | category | flops | bytes accessed | tf_op | source)
XLA Modules:
  0.0 653.6 jit_solution(17117820065498324245)
XLA Ops:
  8.6 5.3 stack.8
  14.0 15.5 %all-to-all-start = ((bf16[128,3,1152,9]{2,1,3,0:T(4,128)(2,1)}), bf16[128,3,1152,9]{2,1,3,0:T(4,128)(2,1)}, u32[]{:S(2)}, u32[]{:S(2)}) async-start(bf16[128,3,1152,9]{2,1,3,0:T(4,128)(2,1)} %stack.8), calls=%async_computation | async-start | bytes 21233664 | tf_op jit(solution)/shard_map/all_to_all | solution.py:128
  32.9 157.5 %all-gather.8.cloned.1.call-done = bf16[128,9,1152]{2,1,0:T(8,128)(2,1)} async-done(((bf16[1,9,1152]{2,1,0:T(8,128)(2,1)}), bf16[128,9,1152]{2,1,0:T(8,128)(2,1)}) %all-gather.8.cloned.1.call-update) | async-done | bytes 2654224 | tf_op jit(solution)/shard_map/all_gather | solution.py:142
  190.4 4.3 reshape.378
  194.7 133.4 %all-gather.10.cloned.1.call-done = bf16[128,9,1152]{2,1,0:T(8,128)(2,1)} async-done(((bf16[1,9,1152]{2,1,0:T(8,128)(2,1)}), bf16[128,9,1152]{2,1,0:T(8,128)(2,1)}) %all-gather.10.cloned.1.call-update) | async-done | bytes 2654224 | tf_op jit(solution)/shard_map/all_gather | solution.py:159
  328.1 5.7 reshape.389
  333.8 6.6 %fusion.10 = bf16[3,1,1,256,1152]{4,3,0,2,1:T(8,128)(2,1)S(1)} fusion(bf16[3,1152,1152]{1,0,2:T(4,128)(2,1)} %bitcast.6, bf16[1,256,1152]{2,1,0:T(8,128)(2,1)S(1)} %get-tuple-element.10, f32[256]{0:T(256)S(1)} %add_rsqrt_fusion.1, f32[1152]{0:T(1024)S(1)} %get-tuple-element.21, f32[1152]{0:T(1024)S(1)} %convert_multiply_fusion.1), kind=kOutput, calls=%fused_computation.9 | convolution fusion | flops 2040791040 | bytes 10332160 | tf_op jit(solution)/shard_map/bfpd,jdk->jbfpk/dot_general | solution.py:124
  347.0 4.9 fusion.166
  351.9 2.8 fusion.61
  356.4 2.5 pad_maximum_fusion
  358.9 8.8 %all-to-all-start.1 = ((bf16[2,1,2,128,1152]{4,2,0,1,3:T(2,128)(2,1)}), bf16[2,1,2,128,1152]{4,2,0,1,3:T(2,128)(2,1)}, u32[]{:S(2)}, u32[]{:S(2)}) async-start(bf16[2,1,2,128,1152]{4,2,0,1,3:T(2,128)(2,1)} %pad_maximum_fusion), calls=%async_computation.1 | async-start | bytes 2359296 | tf_op jit(solution)/shard_map/all_to_all | solution.py:152
  367.8 92.9 %all-gather.6.cloned.1.call-done = bf16[3,1152,1152]{1,0,2:T(4,128)(2,1)} async-done(((bf16[3,1152,9]{1,0,2:T(4,128)(2,1)}), bf16[3,1152,1152]{1,0,2:T(4,128)(2,1)}) %all-gather.6.cloned.1.call-update) | async-done | bytes 7962640 | tf_op jit(solution)/shard_map/all_gather | solution.py:158
  460.7 24.0 %fusion.163 = (bf16[1,1152,1152]{1,0,2:T(2,128)(2,1)}, bf16[1,1152,1152]{1,0,2:T(2,128)(2,1)}, bf16[1,1152,1152]{1,0,2:T(2,128)(2,1)}) fusion(bf16[3,1152,1152]{1,0,2:T(4,128)(2,1)} %all-gather.6.cloned.1.call-done), kind=kLoop, calls=%fused_computation.173 | loop fusion | bytes 15925248 | tf_op jit(solution)/shard_map/jvp()/slice | solution.py:192
  484.7 10.9 %copy.107 = bf16[1,1152,1152]{2,1,0:T(8,128)(2,1)S(1)} copy(bf16[1,1152,1152]{1,0,2:T(2,128)(2,1)} %get-tuple-element.11) | data formatting | bytes 5308416
  495.6 12.2 %copy.108 = bf16[1,1152,1152]{2,1,0:T(8,128)(2,1)} copy(bf16[1,1152,1152]{1,0,2:T(2,128)(2,1)} %get-tuple-element.13) | data formatting | bytes 5308416
  507.8 12.2 %copy.106 = bf16[1,1152,1152]{2,1,0:T(8,128)(2,1)} copy(bf16[1,1152,1152]{1,0,2:T(2,128)(2,1)} %get-tuple-element.12) | data formatting | bytes 5308416
  524.5 2.8 reshape.368
  527.3 2.9 fusion.37
  530.3 2.9 reshape.369
  533.2 3.6 fusion.68
  536.7 2.6 fusion.167
  539.3 2.6 slice_convert_fusion
  542.0 2.9 fusion.31
  544.8 3.7 reshape.367
  548.5 3.9 fusion.59
  552.4 2.9 copy.88
  555.3 2.9 reshape.370
  558.3 3.2 fusion.41
  563.1 3.1 collective-permute-start
  566.8 5.5 collective-permute-done
  573.7 3.4 fusion.29
  617.6 27.2 %all_to_all.29 = bf16[2,64,2,1152]{3,2,0,1:T(2,128)(2,1)S(1)} all-to-all(bf16[2,64,2,1152]{3,2,0,1:T(2,128)(2,1)S(1)} %copy.98), channel_id=1, replica_groups=mesh['cfg'=2,'seq'=64,'clip'=2] {'seq'}, dimensions={1} | all-to-all | bytes 1179648 | tf_op jit(solution)/shard_map/all_to_all | solution.py:205
  (145 shorter events, 61.9 us)
Async XLA Ops:
  7.2 183.2 %all-gather.8.cloned.1.call-start = ((), (), s32[]{:S(2)}) async-start(), calls=%async_computation.4 | async-start | bytes 4755456 | tf_op jit(solution)/shard_map/all_gather | solution.py:142
  7.9 320.2 %all-gather.10.cloned.1.call-start = ((), (), s32[]{:S(2)}) async-start(), calls=%async_computation.5 | async-start | bytes 4755456 | tf_op jit(solution)/shard_map/all_gather | solution.py:159
  13.9 17.0 %copy-start.37 = (bf16[1152]{0:T(1024)(128)(2,1)S(1)}, bf16[1152]{0:T(1024)(128)(2,1)}, u32[]{:S(2)}) copy-start(bf16[1152]{0:T(1024)(128)(2,1)} %param.19) | copy-start | bytes 6916
  13.9 17.0 %copy-start.38 = (bf16[1152]{0:T(1024)(128)(2,1)S(1)}, bf16[1152]{0:T(1024)(128)(2,1)}, u32[]{:S(2)}) copy-start(bf16[1152]{0:T(1024)(128)(2,1)} %param.17) | copy-start | bytes 6916
  13.9 17.0 %copy-start.39 = (bf16[1152]{0:T(1024)(128)(2,1)S(1)}, bf16[1152]{0:T(1024)(128)(2,1)}, u32[]{:S(2)}) copy-start(bf16[1152]{0:T(1024)(128)(2,1)} %param.18) | copy-start | bytes 6916
  13.9 17.0 %copy-start.23 = (bf16[1,256,1152]{2,1,0:T(8,128)(2,1)S(1)}, bf16[1,256,1152]{2,1,0:T(8,128)(2,1)}, u32[]{:S(2)}) copy-start(bf16[1,256,1152]{2,1,0:T(8,128)(2,1)} %param.14) | copy-start | bytes 1769476
  14.0 17.0 %copy-start.24 = (bf16[1,256,1152]{2,1,0:T(8,128)(2,1)S(1)}, bf16[1,256,1152]{2,1,0:T(8,128)(2,1)}, u32[]{:S(2)}) copy-start(bf16[1,256,1152]{2,1,0:T(8,128)(2,1)} %param.13) | copy-start | bytes 1769476
  14.0 319.9 %all-to-all-start = ((bf16[128,3,1152,9]{2,1,3,0:T(4,128)(2,1)}), bf16[128,3,1152,9]{2,1,3,0:T(4,128)(2,1)}, u32[]{:S(2)}, u32[]{:S(2)}) async-start(bf16[128,3,1152,9]{2,1,3,0:T(4,128)(2,1)} %stack.8), calls=%async_computation | async-start | bytes 21233664 | tf_op jit(solution)/shard_map/all_to_all | solution.py:128
  29.5 431.2 %all-gather.6.cloned.1.call-start = ((), (), s32[]{:S(2)}) async-start(), calls=%async_computation.3 | async-start | bytes 10699776 | tf_op jit(solution)/shard_map/all_gather | solution.py:158
  31.4 302.4 %copy-start.15 = (bf16[1,256,1152]{2,1,0:T(8,128)(2,1)}, bf16[1,256,1152]{2,1,0:T(8,128)(2,1)S(1)}, u32[]{:S(2)}) copy-start(bf16[1,256,1152]{2,1,0:T(8,128)(2,1)S(1)} %get-tuple-element.10) | copy-start | bytes 1769476
  347.0 4.9 copy-start.22
  351.9 2.8 copy-start.16
  358.9 161.1 %all-to-all-start.1 = ((bf16[2,1,2,128,1152]{4,2,0,1,3:T(2,128)(2,1)}), bf16[2,1,2,128,1152]{4,2,0,1,3:T(2,128)(2,1)}, u32[]{:S(2)}, u32[]{:S(2)}) async-start(bf16[2,1,2,128,1152]{4,2,0,1,3:T(2,128)(2,1)} %pad_maximum_fusion), calls=%async_computation.1 | async-start | bytes 2359296 | tf_op jit(solution)/shard_map/all_to_all | solution.py:152
  539.3 2.7 copy-start
  563.1 9.2 %collective-permute-start = (bf16[64,2,1152]{2,0,1:T(8,128)(2,1)}, bf16[64,2,1152]{2,0,1:T(8,128)(2,1)S(1)}, u32[]{:S(2)}, u32[]{:S(2)}) collective-permute-start(bf16[64,2,1152]{2,0,1:T(8,128)(2,1)} %dynamic-slice_bitcast_fusion), channel_id=1, source_target_pairs={{0,128},{128,0},{1,129},{129,1},{2,130},{130,2},{3,131},{131,3},{4... | collective-permute-start | bytes 884744 | tf_op jit(solution)/shard_map/ppermute | solution.py:13
  573.7 3.4 copy-start.9
  573.7 7.6 %copy-start.29 = (f32[64,2]{0,1:T(2,128)}, f32[64,2]{0,1:T(2,128)S(1)}, u32[]{:S(2)}) copy-start(f32[64,2]{0,1:T(2,128)S(1)} %get-tuple-element.23) | copy-start | bytes 1540
  573.7 3.6 copy-start.2
  584.7 4.3 copy-start.13
  587.1 7.1 %copy-start.11 = (f32[64,2,1152]{2,0,1:T(8,128)S(1)}, f32[64,2,1152]{2,0,1:T(8,128)}, u32[]{:S(2)}) copy-start(f32[64,2,1152]{2,0,1:T(8,128)} %fusion.23) | copy-start | bytes 1769476
  598.5 2.6 copy-start.7
  598.5 2.6 copy-start.27
  598.9 2.1 copy-start.25
  599.3 2.1 copy-start.31
  601.0 3.9 copy-start.3
  607.2 3.7 copy-start.28
  607.2 3.7 copy-start.34
  610.9 2.0 copy-start.8
  610.9 2.1 copy-start.26
  610.9 2.1 copy-start.32
  610.9 2.1 copy-start.36
  613.1 2.2 copy-start.10
  (14 other events, 20.2 us)
Sparse Core Ops, SparseCore 0:
  11.7 178.6 all-gather.7
  194.1 133.9 all-gather.9
  331.7 128.9 all-gather.5
